TPU v7x, 256 devices: a whole 4x4x8 slice. The times are simulated.
256 devices in a mesh: band: 8 (over z), dev: 32 (over x, y, core).
Axes of the slice: x: 4, y: 4, z: 8, core: 2. Of those that a mesh axis runs over, the one named last changes fastest.
Arguments:
- anomaly: float32 [256, 1048576], P('dev', 'band'), may hold values from -6 to 6
- ocean_mask: int32 [1048576], P('band'), may hold values 0 or 1
- area_weight: float32 [1048576], P('band'), may hold values from 0.02 to 1
Outputs:
- factor: float32 [256, 256], replicated
- scores: float32 [256, 1048576], P(None, ('band', 'dev'))
All inputs are finite; a program needn't handle non-finite values. No bound on the sum of `ocean_mask` on one device may be relied on, other than what follows from the above.
Results may differ from a plain program's by a relative error of at most 0.000075.
Values sent between devices are 32-bit elements; how exact they have to be, the bound alone decides.
A program may use at most 64 MiB of HBM per device.

v0:
```python
import jax
import jax.numpy as jnp
from jax import lax
from jax.sharding import PartitionSpec as P


def on_device(anomaly, ocean_mask, area_weight):
    weights = area_weight * ocean_mask.astype(jnp.float32)
    local_scaled = anomaly * jnp.sqrt(weights)[None, :]
    group_size = lax.axis_size("dev")
    own_cells = weights.shape[0] // group_size
    own_weights = lax.dynamic_slice_in_dim(weights, lax.axis_index("dev") * own_cells, own_cells, 0)
    partial_total = jnp.sum(own_weights)
    scaled = lax.all_to_all(local_scaled, "dev", split_axis=1, concat_axis=0, tiled=True)
    partial_gram = jnp.dot(scaled, scaled.T, precision=lax.Precision.HIGHEST)
    gram, total = lax.psum((partial_gram, partial_total), ("band", "dev"))
    lower = jnp.linalg.cholesky(gram / total)
    scores = lax.linalg.triangular_solve(lower, scaled, left_side=True, lower=True)
    return (lower.T, scores)


def solution(mesh):
    return jax.shard_map(
        on_device,
        mesh=mesh,
        in_specs=(P("dev", "band"), P("band"), P("band")),
        out_specs=(P(), P(None, ("band", "dev"))),
        check_vma=False,
    )
```

profile of v0, /device:TPU:2, one launch (start us, length us, event | category | flops | bytes accessed | tf_op | source)
XLA Modules:
  0.0 410.5 jit_solution(14869644310885381661)
XLA Ops:
  7.2 0.0 all-reduce.3.cloned.1.call-start
  7.2 1.4 fusion.11
  8.6 2.7 broadcast_multiply_fusion
  11.3 55.5 %all_to_all.19 = f32[8,32,4096]{2,0,1:T(8,128)S(1)} all-to-all(f32[8,32,4096]{2,0,1:T(8,128)S(1)} %bitcast.48), channel_id=1, replica_groups=mesh['band'=8,'dev'=32] {'dev'}, dimensions={1} | all-to-all | bytes 8388608 | tf_op jit(solution)/shard_map/all_to_all | solution.py:14
  66.8 0.0 copy-start
  66.8 2.0 copy-done
  68.9 4.2 %fusion = f32[256,256]{0,1:T(8,128)} fusion(f32[8,32,4096]{2,0,1:T(8,128)S(1)} %all_to_all.19), kind=kOutput, calls=%fused_computation.4 | convolution fusion | flops 3221225472 | bytes 4456448 | tf_op jit(solution)/shard_map/dot_general | solution.py:15
  73.1 0.0 all-reduce.3.cloned.1.call-update
  73.1 0.6 dynamic-slice_reduce_fusion
  73.7 80.0 %psum.15 = f32[]{:T(128)} all-reduce(f32[]{:T(128)} %dynamic-slice_reduce_fusion), channel_id=1, replica_groups=mesh['band'=8,'dev'=32] {'band','dev'}, use_global_device_ids=true, to_apply=%region_2.0 | all-reduce | flops 1 | bytes 8 | tf_op jit(solution)/shard_map/psum | solution.py:16
  153.8 175.7 %all-reduce.3.cloned.1.call-done = f32[256,256]{0,1:T(8,128)} async-done(((f32[256,256]{0,1:T(8,128)}), f32[256,256]{0,1:T(8,128)}) %all-reduce.3.cloned.1.call-update) | async-done | bytes 262160 | tf_op jit(solution)/shard_map/psum | solution.py:16
  329.5 1.6 broadcast_divide_fusion
  331.1 0.1 copy.6
  331.2 1.6 fusion.3
  332.8 11.7 %cholesky.50 = f32[128,128]{1,0:T(8,128)S(1)} custom-call(f32[128,128]{1,0:T(8,128)S(1)} %cholesky.118), custom_call_target="Cholesky" | custom-call | tf_op jit(solution)/shard_map/jit(cholesky)/cholesky | solution.py:17
  344.6 9.8 %custom-call.14 = f32[1,128,128]{1,2,0:T(8,128)S(1)} custom-call(f32[1,128,128]{2,1,0:T(8,128)S(1)} %get-tuple-element.29), custom_call_target="InvertDiagBlocksLowerTriangular" | custom-call | tf_op jit(solution)/shard_map/jit(cholesky)/cholesky | solution.py:17
  354.4 0.2 constant_dynamic-update-slice_fusion.1
  354.6 0.3 convolution_subtract_fusion.1
  354.9 11.7 %cholesky.105 = f32[128,128]{1,0:T(8,128)S(1)} custom-call(f32[128,128]{1,0:T(8,128)S(1)} %convolution_subtract_fusion.1), custom_call_target="Cholesky" | custom-call | tf_op jit(solution)/shard_map/jit(cholesky)/cholesky | solution.py:17
  366.7 0.7 compare_reduce_fusion
  368.8 0.8 copy.7
  369.6 0.1 triangular_solve.46
  369.7 4.1 while.1
  369.7 0.7 fusion.18
  370.4 1.3 bitcast_dynamic-update-slice_fusion.2
  371.7 0.7 fusion.18
  372.4 1.3 bitcast_dynamic-update-slice_fusion.2
  373.8 19.9 %custom-call.15 = f32[2,128,128]{1,2,0:T(8,128)S(1)} custom-call(f32[2,128,128]{2,1,0:T(8,128)S(1)} %get-tuple-element.9), custom_call_target="InvertDiagBlocksLowerTriangular" | custom-call | tf_op jit(solution)/shard_map/triangular_solve | solution.py:18
  393.7 0.0 copy-start.1
  393.7 3.6 fusion.2
  397.3 0.0 copy-done.1
  397.3 1.9 convolution_subtract_fusion
  399.3 1.9 fusion.7
  401.2 2.5 pad_maximum_fusion
  (9 shorter events, 0.2 us)
Async XLA Ops:
  7.2 322.3 %all-reduce.3.cloned.1.call-start = ((), (), s32[]{:S(2)}) async-start(), calls=%async_computation.1 | async-start | bytes 524288 | tf_op jit(solution)/shard_map/psum | solution.py:16
  66.8 2.0 copy-start
  393.7 3.7 copy-start.1
Sparse Core Ops, SparseCore 0:
  73.2 256.1 all-reduce.2
where the time goes:
time: 411 us
  waiting for transfers between devices  176 us (43%)
  blocking collectives  136 us (33%)
  other arithmetic  64.4 us (16%)
  between operations  15.5 us (4%)
  matrix products  12.2 us (3%)
  local copies, waits for them, and re-layouts  7.1 us (2%)
    psum x1, waiting for transfers between devices, on_device(): gram, total = lax.psum((partial_gram, partial_total), ('band', 'dev'))  176 us
    psum x1, blocking collectives, on_device(): gram, total = lax.psum((partial_gram, partial_total), ('band', 'dev'))  80 us
    all_to_all x1, blocking collectives, on_device(): lax.all_to_all(local_scaled, 'dev', split_axis=1, concat_axis=0, tiled=True)  55.5 us
    another operation x6, other arithmetic, on_device(): lower = jnp.linalg.cholesky(gram / total)  34 us
    another operation x4, other arithmetic, on_device(): lax.linalg.triangular_solve(lower, scaled, left_side=True, lower=True)  22.4 us
  transfers between devices with their start and end apart: 1, of which 1 were waited for; matrix products, arithmetic and copies ran while one was open for 0% of the time, Pallas kernels for 0%

commit v1 on v0

--- a/solution.py
+++ b/solution.py
@@ -13,7 +13,7 @@
     partial_total = jnp.sum(own_weights)
     scaled = lax.all_to_all(local_scaled, "dev", split_axis=1, concat_axis=0, tiled=True)
     partial_gram = jnp.dot(scaled, scaled.T, precision=lax.Precision.HIGHEST)
-    gram, total = lax.psum((partial_gram, partial_total), ("band", "dev"))
+    gram, total = lax.psum(lax.psum((partial_gram, partial_total), "dev"), "band")
     lower = jnp.linalg.cholesky(gram / total)
     scores = lax.linalg.triangular_solve(lower, scaled, left_side=True, lower=True)
     return (lower.T, scores)

time: 411 us -> 353 us (0.86)
  the two profiles are of different devices: /device:TPU:2 before, /device:TPU:0 now
where the time goes in v1:
time: 353 us; the launch traced here: 352 us
  blocking collectives  141 us (40%)
  waiting for transfers between devices  112 us (32%)
  other arithmetic  64.4 us (18%)
  between operations  15.5 us (4%)
  matrix products  12.2 us (3%)
  local copies, waits for them, and re-layouts  7.1 us (2%)
    psum x1, waiting for transfers between devices, on_device(): lax.psum((partial_gram, partial_total), 'dev')  112 us
    psum x1, blocking collectives, on_device(): lax.psum((partial_gram, partial_total), 'dev')  66.7 us
    all_to_all x1, blocking collectives, on_device(): lax.all_to_all(local_scaled, 'dev', split_axis=1, concat_axis=0, tiled=True)  55.9 us
    another operation x6, other arithmetic, on_device(): lower = jnp.linalg.cholesky(gram / total)  34 us
    another operation x4, other arithmetic, on_device(): lax.linalg.triangular_solve(lower, scaled, left_side=True, lower=True)  22.4 us
    psum x1, blocking collectives, on_device(): lax.psum(lax.psum((partial_gram, partial_total), 'dev'), 'band')  18.3 us
    another operation x3, matrix products, on_device(): lax.linalg.triangular_solve(lower, scaled, left_side=True, lower=True)  7.51 us
  transfers between devices with their start and end apart: 2, of which 1 were waited for; matrix products, arithmetic and copies ran while one was open for 0% of the time, Pallas kernels for 0%

profile of v1, /device:TPU:0, one launch (start us, length us, event | category | flops | bytes accessed | tf_op | source)
XLA Modules:
  0.0 352.4 jit_solution(15414415743833680613)
XLA Ops:
  7.2 0.0 all-reduce.4.cloned.1.call-start
  7.2 1.4 fusion.11
  8.6 2.7 broadcast_multiply_fusion
  11.3 55.9 %all_to_all.19 = f32[8,32,4096]{2,0,1:T(8,128)S(1)} all-to-all(f32[8,32,4096]{2,0,1:T(8,128)S(1)} %bitcast.48), channel_id=1, replica_groups=mesh['band'=8,'dev'=32] {'dev'}, dimensions={1} | all-to-all | bytes 8388608 | tf_op jit(solution)/shard_map/all_to_all | solution.py:14
  67.2 0.0 copy-start
  67.2 2.0 copy-done
  69.2 4.2 %fusion = f32[256,256]{0,1:T(8,128)} fusion(f32[8,32,4096]{2,0,1:T(8,128)S(1)} %all_to_all.19), kind=kOutput, calls=%fused_computation.4 | convolution fusion | flops 3221225472 | bytes 4456448 | tf_op jit(solution)/shard_map/dot_general | solution.py:15
  73.5 0.0 all-reduce.4.cloned.1.call-update
  73.5 0.0 all-reduce.6.cloned.1.call-start
  73.5 112.2 %all-reduce.4.cloned.1.call-done = f32[256,256]{0,1:T(8,128)} async-done(((f32[256,256]{0,1:T(8,128)}), f32[256,256]{0,1:T(8,128)}) %all-reduce.4.cloned.1.call-update) | async-done | bytes 262160 | tf_op jit(solution)/shard_map/psum | solution.py:16
  185.7 0.0 all-reduce.6.cloned.1.call-update
  185.7 0.6 dynamic-slice_reduce_fusion
  186.3 66.7 %psum.30 = f32[]{:T(128)} all-reduce(f32[]{:T(128)} %dynamic-slice_reduce_fusion), channel_id=1, replica_groups=mesh['band'=8,'dev'=32] {'dev'}, use_global_device_ids=true, to_apply=%region_3.0 | all-reduce | flops 1 | bytes 8 | tf_op jit(solution)/shard_map/psum | solution.py:16
  253.0 18.3 %psum.31 = f32[]{:T(128)} all-reduce(f32[]{:T(128)} %psum.30), channel_id=1, replica_groups=mesh['band'=8,'dev'=32] {'band'}, use_global_device_ids=true, to_apply=%region_4.0 | all-reduce | flops 1 | bytes 8 | tf_op jit(solution)/shard_map/psum | solution.py:16
  271.3 0.0 all-reduce.6.cloned.1.call-done
  271.3 1.6 broadcast_divide_fusion
  272.9 0.1 copy.6
  273.0 1.6 fusion.3
  274.7 11.7 %cholesky.50 = f32[128,128]{1,0:T(8,128)S(1)} custom-call(f32[128,128]{1,0:T(8,128)S(1)} %cholesky.118), custom_call_target="Cholesky" | custom-call | tf_op jit(solution)/shard_map/jit(cholesky)/cholesky | solution.py:17
  286.4 9.8 %custom-call.14 = f32[1,128,128]{1,2,0:T(8,128)S(1)} custom-call(f32[1,128,128]{2,1,0:T(8,128)S(1)} %get-tuple-element.29), custom_call_target="InvertDiagBlocksLowerTriangular" | custom-call | tf_op jit(solution)/shard_map/jit(cholesky)/cholesky | solution.py:17
  296.3 0.2 constant_dynamic-update-slice_fusion.1
  296.5 0.3 convolution_subtract_fusion.1
  296.8 11.7 %cholesky.105 = f32[128,128]{1,0:T(8,128)S(1)} custom-call(f32[128,128]{1,0:T(8,128)S(1)} %convolution_subtract_fusion.1), custom_call_target="Cholesky" | custom-call | tf_op jit(solution)/shard_map/jit(cholesky)/cholesky | solution.py:17
  308.5 0.7 compare_reduce_fusion
  310.6 0.8 copy.7
  311.5 0.1 triangular_solve.46
  311.5 4.1 %while.1 = (s32[]{:T(128)}, f32[256,256]{1,0:T(8,128)S(1)}, s32[2,2]{1,0:T(2,128)S(1)}, f32[2,128,128]{2,1,0:T(8,128)S(1)}, s32[]{:T(128)}) while((s32[]{:T(128)}, f32[256,256]{1,0:T(8,128)S(1)}, s32[2,2]{1,0:T(2,128)S(1)}, f32[2,128,128]{2,1,0:T(8,128)S(1)}, s32[]{:T(128)}) %tuple.30), condition=%wide.while_cond, body=%wide.while_body.sunk | while | flops 2 | bytes 131189 | solution.py:18
  311.5 0.7 fusion.18
  312.2 1.3 bitcast_dynamic-update-slice_fusion.2
  313.6 0.7 fusion.18
  314.2 1.3 bitcast_dynamic-update-slice_fusion.2
  315.6 19.9 %custom-call.15 = f32[2,128,128]{1,2,0:T(8,128)S(1)} custom-call(f32[2,128,128]{2,1,0:T(8,128)S(1)} %get-tuple-element.9), custom_call_target="InvertDiagBlocksLowerTriangular" | custom-call | tf_op jit(solution)/shard_map/triangular_solve | solution.py:18
  335.5 0.0 copy-start.1
  335.5 3.6 %fusion.2 = f32[128,4096]{1,0:T(8,128)S(1)} fusion(f32[32,8,4096]{2,1,0:T(8,128)} %bitcast.46, f32[2,128,128]{1,2,0:T(8,128)S(1)} %custom-call.15), kind=kOutput, calls=%fused_computation.8 | convolution fusion | flops 805306368 | bytes 4259840 | tf_op jit(solution)/shard_map/triangular_solve | solution.py:18
  339.2 0.0 copy-done.1
  339.2 1.9 convolution_subtract_fusion
  341.1 1.9 fusion.7
  343.1 2.5 pad_maximum_fusion
  (9 shorter events, 0.2 us)
Async XLA Ops:
  7.2 178.5 %all-reduce.4.cloned.1.call-start = ((), (), s32[]{:S(2)}) async-start(), calls=%async_computation.1 | async-start | bytes 524288 | tf_op jit(solution)/shard_map/psum | solution.py:16
  67.2 2.0 copy-start
  73.5 197.8 %all-reduce.6.cloned.1.call-start = ((), (), s32[]{:S(2)}) async-start(), calls=%async_computation.2 | async-start | bytes 524288 | tf_op jit(solution)/shard_map/psum | solution.py:16
  335.5 3.7 %copy-start.1 = (f32[8,32,4096]{2,0,1:T(8,128)S(1)}, f32[8,32,4096]{2,0,1:T(8,128)}, u32[]{:S(2)}) copy-start(f32[8,32,4096]{2,0,1:T(8,128)} %copy-done) | copy-start | bytes 12582916
Sparse Core Ops, SparseCore 0:
  73.6 112.0 all-reduce.3
  188.0 72.6 all-reduce.5
